TPU v7x, 256 devices: a whole 4x4x8 slice. The times are simulated.
256 devices in a mesh: lane: 8 (over y, core), node: 32 (over x, z).
Axes of the slice: x: 4, y: 4, z: 8, core: 2. Of those that a mesh axis runs over, the one named last changes fastest.
Arguments:
- source_row: int32 [32768], P(('lane', 'node')), may hold values from 0 to 63, as said below
- time_bucket: int32 [32768], P(('lane', 'node')), may hold values from 0 to 4095
- neighbour_slot: int32 [32768, 10], P(('lane', 'node')), may hold values from 0 to 511, as said below
- neighbour_age: int32 [32768, 10], P(('lane', 'node')), may hold values from 0 to 4095
- neighbour_count: int32 [32768], P(('lane', 'node')), may hold values from 1 to 10, as said below
- request_rows: int32 [8192, 16], P(('lane', 'node')), may hold values from 0 to 63, as said below
- memory_start: float32 [2048, 512], P('node'), may hold values from -6 to 6
- decay_rate: float32 [512], replicated, may hold values from 0.02 to 1
- time_frequency: float32 [128], replicated, may hold values from 0.0005 to 0.5
- time_phase: float32 [128], replicated, may hold values from -3.140625 to 3.140625
- weight_message: float32 [128, 512], replicated, may hold values from -0.5 to 0.5
- weight_query: bfloat16 [512, 1024], replicated, may hold values from -0.25 to 0.25
- weight_keyval: bfloat16 [512, 2048], replicated, may hold values from -0.25 to 0.25
- weight_time: bfloat16 [128, 1024], replicated, may hold values from -0.5 to 0.5
- weight_output: bfloat16 [1024, 1024], replicated, may hold values from -0.1875 to 0.1875
- weight_skip: bfloat16 [512, 1024], replicated, may hold values from -0.25 to 0.25
Outputs:
- embedding: bfloat16 [32768, 1024], P(('lane', 'node'))
- lane_memory: float32 [8, 2048, 512], P('lane', 'node')
Inputs may be any that keep to these rules, and one draw needn't show every extreme that they name: `source_row`: every row of a device's partition is the source of at least one of that device's events. Each list of request_rows holds 16 different rows; for each device the lists of the owners are what its neighbour slots refer to, filled in a prefix, and at least one list of every device is used in full. neighbour_slot % 16 lies inside the used prefix of the owner's list of the same device. `neighbour_count`: every device has an event with all 10 neighbours.
All inputs are finite; a program needn't handle non-finite values.
Results may differ from a plain program's by a relative error of at most 0.024.
Values may be sent and summed in bfloat16 or wider, within the bound.
A program may use at most 64 MiB of HBM per device.

v0:
```python
import jax
import jax.numpy as jnp
from jax import lax
from jax.sharding import PartitionSpec as P

H = 8


def shortened(value):

    def short(part):
        return part.astype(jnp.bfloat16) if part.dtype == jnp.float32 else part

    return jax.tree.map(short, value)


def from_behind(value, axis, steps):
    count = lax.axis_size(axis)
    leading, last = (max(0, -steps), min(count, count - steps))
    return lax.ppermute(value, axis, [(source, source + steps) for source in range(leading, last)])


def encode(values, time_frequency, time_phase):
    return jnp.cos(values.astype(jnp.float32)[..., None] * time_frequency + time_phase)


def attend(query, own, far, time_keys, counts, width, heads):
    events, neighbours = (far.shape[0], far.shape[1])
    size = width // heads
    keys = (far[:, :, :width].astype(jnp.float32) + time_keys).astype(jnp.bfloat16)
    values = far[:, :, width:]
    query_heads = query.reshape(events, heads, size)
    key_heads = keys.reshape(events, neighbours, heads, size)
    value_heads = values.reshape(events, neighbours, heads, size)
    own_keys = own[:, :width].reshape(events, heads, size)
    own_values = own[:, width:].reshape(events, heads, size)
    scale = 1.0 / jnp.sqrt(jnp.float32(size))
    scores = (
        jnp.einsum("ehd,ekhd->ehk", query_heads, key_heads, preferred_element_type=jnp.float32)
        * scale
    )
    selfish = (
        jnp.einsum("ehd,ehd->eh", query_heads, own_keys, preferred_element_type=jnp.float32) * scale
    )
    valid = jnp.arange(neighbours, dtype=jnp.int32)[None, None, :] < counts[:, None, None]
    scores = jnp.where(valid, scores, -1e30)
    largest = jnp.maximum(jnp.max(scores, axis=-1), selfish)
    expo = jnp.where(valid, jnp.exp(scores - largest[..., None]), 0.0)
    expo_self = jnp.exp(selfish - largest)
    total = jnp.sum(expo, axis=-1) + expo_self
    weights = (expo / total[..., None]).astype(jnp.bfloat16)
    weight_self = (expo_self / total).astype(jnp.bfloat16)
    mixed = jnp.einsum("ehk,ekhd->ehd", weights, value_heads, preferred_element_type=jnp.float32)
    mixed = mixed + weight_self.astype(jnp.float32)[..., None] * own_values.astype(jnp.float32)
    return mixed.reshape(events, width).astype(jnp.bfloat16)


def local(
    source_row,
    time_bucket,
    neighbour_slot,
    neighbour_age,
    neighbour_count,
    request_rows,
    memory_start,
    decay_rate,
    time_frequency,
    time_phase,
    weight_message,
    weight_query,
    weight_keyval,
    weight_time,
    weight_output,
    weight_skip,
):
    owned, channels = memory_start.shape
    events, neighbours = neighbour_slot.shape
    width = weight_query.shape[1]
    messages = jnp.dot(
        encode(time_bucket, time_frequency, time_phase),
        weight_message,
        precision=lax.Precision.HIGHEST,
    )
    member = (source_row[None, :] == jnp.arange(owned, dtype=jnp.int32)[:, None]).astype(
        jnp.float32
    )
    touches = jnp.sum(member, axis=1)
    summed = jnp.dot(member, messages, precision=lax.Precision.HIGHEST)
    ownpair = (touches, summed)
    blank = (jnp.zeros_like(touches), jnp.zeros_like(summed))
    carried = blank
    for hopping in range(lax.axis_size("lane") - 1):
        carried = from_behind(
            shortened(
                (
                    carried[0] + ownpair[0],
                    jnp.exp(-decay_rate[None, :] * ownpair[0][:, None]) * carried[1] + ownpair[1],
                )
            ),
            "lane",
            1,
        )
    memory_before = jnp.exp(-decay_rate[None, :] * carried[0][:, None]) * memory_start + carried[1]
    memory_after = jnp.exp(-decay_rate[None, :] * touches[:, None]) * memory_before + summed
    rows = memory_before.astype(jnp.bfloat16)
    query_in = jnp.take(rows, source_row, axis=0)
    query = jnp.dot(query_in, weight_query, preferred_element_type=jnp.float32).astype(jnp.bfloat16)
    own = jnp.dot(query_in, weight_keyval, preferred_element_type=jnp.float32).astype(jnp.bfloat16)
    asked = lax.all_to_all(request_rows, "node", split_axis=0, concat_axis=0, tiled=True)
    outgoing = jnp.take(rows, asked.reshape(-1), axis=0).reshape(asked.shape + (channels,))
    block = lax.all_to_all(outgoing, "node", split_axis=0, concat_axis=0, tiled=True)
    flat = block.reshape(-1, channels)
    made = jnp.dot(flat, weight_keyval, preferred_element_type=jnp.float32).astype(jnp.bfloat16)
    received = made.reshape(block.shape[0], block.shape[1], 2 * width)
    far = jnp.take(received.reshape(-1, 2 * width), neighbour_slot.reshape(-1), axis=0).reshape(
        events, neighbours, 2 * width
    )
    enc_ages = (
        encode(neighbour_age, time_frequency, time_phase)
        .astype(jnp.bfloat16)
        .reshape(events * neighbours, -1)
    )
    time_keys = jnp.dot(enc_ages, weight_time, preferred_element_type=jnp.float32).reshape(
        events, neighbours, width
    )
    attended = attend(query, own, far, time_keys, neighbour_count, width, H)
    result = jnp.dot(attended, weight_output, preferred_element_type=jnp.float32) + jnp.dot(
        query_in, weight_skip, preferred_element_type=jnp.float32
    )
    return (result.astype(jnp.bfloat16), memory_after[None])


def solution(mesh):
    return jax.shard_map(
        local,
        mesh=mesh,
        in_specs=(
            P(("lane", "node")),
            P(("lane", "node")),
            P(("lane", "node"), None),
            P(("lane", "node"), None),
            P(("lane", "node")),
            P(("lane", "node"), None),
            P("node", None),
            P(),
            P(),
            P(),
            P(),
            P(),
            P(),
            P(),
            P(),
            P(),
        ),
        out_specs=(P(("lane", "node"), None), P("lane", "node", None)),
        check_vma=False,
    )
```

profile of v0, /device:TPU:1, one launch (start us, length us, event | category | flops | bytes accessed | tf_op | source)
XLA Modules:
  0.0 160.5 jit_solution(9282920120100246397)
XLA Ops:
  2.9 1.6 %fusion.16 = f32[128,512]{1,0:T(8,128)S(1)} fusion(f32[128,512]{1,0:T(8,128)} %param.26, f32[128]{0:T(128)} %param.25, f32[128]{0:T(128)} %param.24, f32[128]{0:T(128)S(1)} %convert_element_type.156), kind=kOutput, calls=%fused_computation.42 | convolution fusion | flops 100696064 | bytes 525824 | tf_op jit(solution)/shard_map/dot_general | solution.py:79
  5.5 4.6 %collective-permute-start.7 = (bf16[64,512]{1,0:T(8,128)(2,1)S(1)}, bf16[64,512]{1,0:T(8,128)(2,1)S(1)}, u32[]{:S(2)}, u32[]{:S(2)}) collective-permute-start(bf16[64,512]{1,0:T(8,128)(2,1)S(1)} %get-tuple-element.8), channel_id=1, source_target_pairs={{0,32},{32,64},{64,96},{96,128},{128,160},{160,192},{192,224},{1,3... | collective-permute-start | bytes 196616 | tf_op jit(solution)/shard_map/ppermute | solution.py:20
  10.1 1.9 %collective-permute-start = (bf16[64]{0:T(256)(128)(2,1)S(1)}, bf16[64]{0:T(256)(128)(2,1)S(1)}, u32[]{:S(2)}, u32[]{:S(2)}) collective-permute-start(bf16[64]{0:T(256)(128)(2,1)S(1)} %convert_element_type.142), channel_id=1, source_target_pairs={{0,32},{32,64},{64,96},{96,128},{128,160},{160,192},{192,224},{1,3... | collective-permute-start | bytes 392 | tf_op jit(solution)/shard_map/ppermute | solution.py:20
  12.0 1.4 copy.26
  13.4 11.0 %all-to-all-start = ((s32[32,1,16]{2,1,0:T(1,128)}), s32[32,1,16]{2,1,0:T(1,128)S(1)}, u32[]{:S(2)}, u32[]{:S(2)}) async-start(s32[32,1,16]{2,1,0:T(1,128)} %bitcast), calls=%async_computation | async-start | bytes 32768 | tf_op jit(solution)/shard_map/all_to_all | solution.py:109
  28.1 3.9 %collective-permute-start.1 = (bf16[64]{0:T(256)(128)(2,1)S(1)}, bf16[64]{0:T(256)(128)(2,1)S(1)}, u32[]{:S(2)}, u32[]{:S(2)}) collective-permute-start(bf16[64]{0:T(256)(128)(2,1)S(1)} %add_convert_fusion.13), channel_id=1, source_target_pairs={{0,32},{32,64},{64,96},{96,128},{128,160},{160,192},{192,224},{1,3... | collective-permute-start | bytes 392 | tf_op jit(solution)/shard_map/ppermute | solution.py:20
  32.7 4.1 %collective-permute-start.2 = (bf16[64]{0:T(256)(128)(2,1)S(1)}, bf16[64]{0:T(256)(128)(2,1)S(1)}, u32[]{:S(2)}, u32[]{:S(2)}) collective-permute-start(bf16[64]{0:T(256)(128)(2,1)S(1)} %add_convert_fusion.12), channel_id=1, source_target_pairs={{0,32},{32,64},{64,96},{96,128},{128,160},{160,192},{192,224},{1,3... | collective-permute-start | bytes 392 | tf_op jit(solution)/shard_map/ppermute | solution.py:20
  37.5 4.1 %collective-permute-start.3 = (bf16[64]{0:T(256)(128)(2,1)S(1)}, bf16[64]{0:T(256)(128)(2,1)S(1)}, u32[]{:S(2)}, u32[]{:S(2)}) collective-permute-start(bf16[64]{0:T(256)(128)(2,1)S(1)} %add_convert_fusion.11), channel_id=1, source_target_pairs={{0,32},{32,64},{64,96},{96,128},{128,160},{160,192},{192,224},{1,3... | collective-permute-start | bytes 392 | tf_op jit(solution)/shard_map/ppermute | solution.py:20
  41.8 1.9 %collective-permute-start.8 = (bf16[64,512]{1,0:T(8,128)(2,1)S(1)}, bf16[64,512]{1,0:T(8,128)(2,1)S(1)}, u32[]{:S(2)}, u32[]{:S(2)}) collective-permute-start(bf16[64,512]{1,0:T(8,128)(2,1)S(1)} %add_convert_fusion.6), channel_id=1, source_target_pairs={{0,32},{32,64},{64,96},{96,128},{128,160},{160,192},{192,224},{1,3... | collective-permute-start | bytes 196616 | tf_op jit(solution)/shard_map/ppermute | solution.py:20
  43.7 3.3 %collective-permute-start.4 = (bf16[64]{0:T(256)(128)(2,1)S(1)}, bf16[64]{0:T(256)(128)(2,1)S(1)}, u32[]{:S(2)}, u32[]{:S(2)}) collective-permute-start(bf16[64]{0:T(256)(128)(2,1)S(1)} %add_convert_fusion.10), channel_id=1, source_target_pairs={{0,32},{32,64},{64,96},{96,128},{128,160},{160,192},{192,224},{1,3... | collective-permute-start | bytes 392 | tf_op jit(solution)/shard_map/ppermute | solution.py:20
  47.2 2.2 %collective-permute-start.9 = (bf16[64,512]{1,0:T(8,128)(2,1)S(1)}, bf16[64,512]{1,0:T(8,128)(2,1)S(1)}, u32[]{:S(2)}, u32[]{:S(2)}) collective-permute-start(bf16[64,512]{1,0:T(8,128)(2,1)S(1)} %add_convert_fusion.5), channel_id=1, source_target_pairs={{0,32},{32,64},{64,96},{96,128},{128,160},{160,192},{192,224},{1,3... | collective-permute-start | bytes 196616 | tf_op jit(solution)/shard_map/ppermute | solution.py:20
  49.4 2.5 %collective-permute-start.5 = (bf16[64]{0:T(256)(128)(2,1)S(1)}, bf16[64]{0:T(256)(128)(2,1)S(1)}, u32[]{:S(2)}, u32[]{:S(2)}) collective-permute-start(bf16[64]{0:T(256)(128)(2,1)S(1)} %add_convert_fusion.9), channel_id=1, source_target_pairs={{0,32},{32,64},{64,96},{96,128},{128,160},{160,192},{192,224},{1,3... | collective-permute-start | bytes 392 | tf_op jit(solution)/shard_map/ppermute | solution.py:20
  52.0 3.1 %collective-permute-start.10 = (bf16[64,512]{1,0:T(8,128)(2,1)S(1)}, bf16[64,512]{1,0:T(8,128)(2,1)S(1)}, u32[]{:S(2)}, u32[]{:S(2)}) collective-permute-start(bf16[64,512]{1,0:T(8,128)(2,1)S(1)} %add_convert_fusion.4), channel_id=1, source_target_pairs={{0,32},{32,64},{64,96},{96,128},{128,160},{160,192},{192,224},{1,3... | collective-permute-start | bytes 196616 | tf_op jit(solution)/shard_map/ppermute | solution.py:20
  55.1 1.9 %collective-permute-start.6 = (bf16[64]{0:T(256)(128)(2,1)S(1)}, bf16[64]{0:T(256)(128)(2,1)S(1)}, u32[]{:S(2)}, u32[]{:S(2)}) collective-permute-start(bf16[64]{0:T(256)(128)(2,1)S(1)} %add_convert_fusion.8), channel_id=1, source_target_pairs={{0,32},{32,64},{64,96},{96,128},{128,160},{160,192},{192,224},{1,3... | collective-permute-start | bytes 392 | tf_op jit(solution)/shard_map/ppermute | solution.py:20
  58.2 3.8 %collective-permute-start.11 = (bf16[64,512]{1,0:T(8,128)(2,1)S(1)}, bf16[64,512]{1,0:T(8,128)(2,1)S(1)}, u32[]{:S(2)}, u32[]{:S(2)}) collective-permute-start(bf16[64,512]{1,0:T(8,128)(2,1)S(1)} %add_convert_fusion.3), channel_id=1, source_target_pairs={{0,32},{32,64},{64,96},{96,128},{128,160},{160,192},{192,224},{1,3... | collective-permute-start | bytes 196616 | tf_op jit(solution)/shard_map/ppermute | solution.py:20
  63.4 4.3 %collective-permute-start.12 = (bf16[64,512]{1,0:T(8,128)(2,1)S(1)}, bf16[64,512]{1,0:T(8,128)(2,1)S(1)}, u32[]{:S(2)}, u32[]{:S(2)}) collective-permute-start(bf16[64,512]{1,0:T(8,128)(2,1)S(1)} %add_convert_fusion.2), channel_id=1, source_target_pairs={{0,32},{32,64},{64,96},{96,128},{128,160},{160,192},{192,224},{1,3... | collective-permute-start | bytes 196616 | tf_op jit(solution)/shard_map/ppermute | solution.py:20
  67.7 1.3 collective-permute-done.12
  69.1 4.3 %collective-permute-start.13 = (bf16[64,512]{1,0:T(8,128)(2,1)S(1)}, bf16[64,512]{1,0:T(8,128)(2,1)S(1)}, u32[]{:S(2)}, u32[]{:S(2)}) collective-permute-start(bf16[64,512]{1,0:T(8,128)(2,1)S(1)} %add_convert_fusion.1), channel_id=1, source_target_pairs={{0,32},{32,64},{64,96},{96,128},{128,160},{160,192},{192,224},{1,3... | collective-permute-start | bytes 196616 | tf_op jit(solution)/shard_map/ppermute | solution.py:20
  73.4 1.3 collective-permute-done.13
  75.5 2.0 %gather_fusion.1 = bf16[512,512]{1,0:T(8,128)(2,1)S(1)} fusion(bf16[64,512]{1,0:T(8,128)(2,1)S(1)} %get-tuple-element.5, s32[1024]{0:T(1024)S(1)} %pad_clamp_fusion.1), kind=kCustom, calls=%fused_computation.1 | custom fusion | bytes 1050624 | tf_op jit(solution)/shard_map/jit(_take)/gather | solution.py:110
  78.4 9.8 %all-to-all-start.1 = ((bf16[32,16,512]{2,1,0:T(8,128)(2,1)}), bf16[32,16,512]{2,1,0:T(8,128)(2,1)}, u32[]{:S(2)}, u32[]{:S(2)}) async-start(bf16[32,16,512]{2,1,0:T(8,128)(2,1)} %broadcast_select_fusion), calls=%async_computation.1 | async-start | bytes 1048576 | tf_op jit(solution)/shard_map/all_to_all | solution.py:111
  89.1 1.6 convolution_convert_fusion.2
  92.6 11.1 %all-to-all-done.1 = bf16[32,16,512]{2,1,0:T(8,128)(2,1)} async-done(((bf16[32,16,512]{2,1,0:T(8,128)(2,1)}), bf16[32,16,512]{2,1,0:T(8,128)(2,1)}, u32[]{:S(2)}, u32[]{:S(2)}) %all-to-all-start.1) | async-done | bytes 524320 | tf_op jit(solution)/shard_map/all_to_all | solution.py:111
  103.7 3.6 %convolution_convert_fusion = bf16[512,2048]{1,0:T(8,128)(2,1)} fusion(bf16[512,512]{1,0:T(8,128)(2,1)} %bitcast.4, bf16[512,2048]{1,0:T(8,128)(2,1)S(1)} %copy-done), kind=kOutput, calls=%fused_computation.9 | convolution fusion | flops 1074790400 | bytes 4718592 | tf_op jit(solution)/shard_map/dot_general | solution.py:113
  107.4 12.8 %gather_fusion.2 = bf16[1280,2048]{1,0:T(8,128)(2,1)} fusion(bf16[512,2048]{1,0:T(8,128)(2,1)} %convolution_convert_fusion, s32[2048]{0:T(1024)S(1)} %pad_clamp_fusion), kind=kCustom, calls=%fused_computation.2 | custom fusion | bytes 10490880 | tf_op jit(solution)/shard_map/jit(_take)/gather | solution.py:115
  120.1 9.6 %gather.20 = bf16[128,10,2048]{2,1,0:T(8,128)(2,1)} reshape(bf16[1280,2048]{1,0:T(8,128)(2,1)} %gather_fusion.2) | data formatting | bytes 10485760 | tf_op jit(solution)/shard_map/jit(_take)/gather | solution.py:115
  129.7 9.5 %copy_select_fusion = bf16[128,10,2048]{2,0,1:T(8,128)(2,1)S(1)} fusion(bf16[128,10,2048]{2,1,0:T(8,128)(2,1)} %gather.20, pred[128,10]{0,1:T(8,128)(4,1)S(1)} %compare_and_fusion.1), kind=kLoop, calls=%fused_computation.3 | loop fusion | flops 2621440 | bytes 10487040 | tf_op jit(solution)/shard_map/jit(_take)/select_n | solution.py:115
  139.2 1.8 %slice.24 = bf16[128,10,1024]{2,0,1:T(8,128)(2,1)} slice(bf16[128,10,2048]{2,0,1:T(8,128)(2,1)S(1)} %copy_select_fusion), slice={[0:128], [0:10], [1024:2048]} | slice | bytes 5242880 | tf_op jit(solution)/shard_map/slice | solution.py:31
  141.1 3.3 %add_convert_fusion = bf16[128,10,1024]{2,0,1:T(8,128)(2,1)S(1)} fusion(bf16[128,10,2048]{2,0,1:T(8,128)(2,1)S(1)} %copy_select_fusion, f32[128]{0:T(128)S(1)} %copy-done.6, f32[128]{0:T(128)S(1)} %copy-done.7, f32[128,10]{0,1:T(8,128)S(1)} %convert_element_type.175, bf16[128,1024]{1,0:T(8,128)(2,1)S(1)} %copy-done.4), kind=kOutput, calls=%fused_computation.4 | convolution fusion | flops 339968000 | bytes 5511168 | tf_op jit(solution)/shard_map/dot_general | solution.py:123
  145.4 3.1 %fusion.2 = f32[128,8,1,10]{3,2,1,0:T(1,128)} fusion(bf16[128,8,128,1]{2,3,1,0:T(2,128)(2,1)S(1)} %copy-done.3, bf16[128,10,8,128]{3,2,0,1:T(8,128)(2,1)S(1)} %bitcast.70), kind=kOutput, calls=%fused_computation.7 | convolution fusion | flops 2621440 | bytes 2924544 | tf_op jit(solution)/shard_map/ehd,ekhd->ehk/dot_general | solution.py:39
  150.3 3.9 %copy.44 = bf16[160,8,8,128]{3,2,1,0:T(8,128)(2,1)} copy(bf16[160,8,8,128]{3,1,2,0:T(8,128)(2,1)} %bitcast.67) | data formatting | bytes 5242880
  154.3 3.9 %fusion = f32[128,8,1,128]{3,2,1,0:T(1,128)S(1)} fusion(bf16[128,8,10,1]{2,3,1,0:T(2,128)(2,1)S(1)} %copy.37, bf16[128,10,8,128]{3,2,0,1:T(8,128)(2,1)} %bitcast.69), kind=kOutput, calls=%fused_computation.5 | convolution fusion | flops 2621440 | bytes 3166208 | tf_op jit(solution)/shard_map/ehk,ekhd->ehd/dot_general | solution.py:53
  (86 shorter events, 20.9 us)
Async XLA Ops:
  0.6 91.0 %copy-start = (bf16[512,2048]{1,0:T(8,128)(2,1)S(1)}, bf16[512,2048]{1,0:T(8,128)(2,1)}, u32[]{:S(2)}) copy-start(bf16[512,2048]{1,0:T(8,128)(2,1)} %param.28) | copy-start | bytes 6291460
  0.6 74.0 %copy-start.5 = (f32[64,512]{1,0:T(8,128)S(1)}, f32[64,512]{1,0:T(8,128)}, u32[]{:S(2)}) copy-start(f32[64,512]{1,0:T(8,128)} %param.22) | copy-start | bytes 393220
  5.5 36.2 %collective-permute-start.7 = (bf16[64,512]{1,0:T(8,128)(2,1)S(1)}, bf16[64,512]{1,0:T(8,128)(2,1)S(1)}, u32[]{:S(2)}, u32[]{:S(2)}) collective-permute-start(bf16[64,512]{1,0:T(8,128)(2,1)S(1)} %get-tuple-element.8), channel_id=1, source_target_pairs={{0,32},{32,64},{64,96},{96,128},{128,160},{160,192},{192,224},{1,3... | collective-permute-start | bytes 196616 | tf_op jit(solution)/shard_map/ppermute | solution.py:20
  10.1 18.0 %collective-permute-start = (bf16[64]{0:T(256)(128)(2,1)S(1)}, bf16[64]{0:T(256)(128)(2,1)S(1)}, u32[]{:S(2)}, u32[]{:S(2)}) collective-permute-start(bf16[64]{0:T(256)(128)(2,1)S(1)} %convert_element_type.142), channel_id=1, source_target_pairs={{0,32},{32,64},{64,96},{96,128},{128,160},{160,192},{192,224},{1,3... | collective-permute-start | bytes 392 | tf_op jit(solution)/shard_map/ppermute | solution.py:20
  13.4 48.6 %all-to-all-start = ((s32[32,1,16]{2,1,0:T(1,128)}), s32[32,1,16]{2,1,0:T(1,128)S(1)}, u32[]{:S(2)}, u32[]{:S(2)}) async-start(s32[32,1,16]{2,1,0:T(1,128)} %bitcast), calls=%async_computation | async-start | bytes 32768 | tf_op jit(solution)/shard_map/all_to_all | solution.py:109
  28.1 4.6 %collective-permute-start.1 = (bf16[64]{0:T(256)(128)(2,1)S(1)}, bf16[64]{0:T(256)(128)(2,1)S(1)}, u32[]{:S(2)}, u32[]{:S(2)}) collective-permute-start(bf16[64]{0:T(256)(128)(2,1)S(1)} %add_convert_fusion.13), channel_id=1, source_target_pairs={{0,32},{32,64},{64,96},{96,128},{128,160},{160,192},{192,224},{1,3... | collective-permute-start | bytes 392 | tf_op jit(solution)/shard_map/ppermute | solution.py:20
  32.7 4.8 %collective-permute-start.2 = (bf16[64]{0:T(256)(128)(2,1)S(1)}, bf16[64]{0:T(256)(128)(2,1)S(1)}, u32[]{:S(2)}, u32[]{:S(2)}) collective-permute-start(bf16[64]{0:T(256)(128)(2,1)S(1)} %add_convert_fusion.12), channel_id=1, source_target_pairs={{0,32},{32,64},{64,96},{96,128},{128,160},{160,192},{192,224},{1,3... | collective-permute-start | bytes 392 | tf_op jit(solution)/shard_map/ppermute | solution.py:20
  37.5 6.2 %collective-permute-start.3 = (bf16[64]{0:T(256)(128)(2,1)S(1)}, bf16[64]{0:T(256)(128)(2,1)S(1)}, u32[]{:S(2)}, u32[]{:S(2)}) collective-permute-start(bf16[64]{0:T(256)(128)(2,1)S(1)} %add_convert_fusion.11), channel_id=1, source_target_pairs={{0,32},{32,64},{64,96},{96,128},{128,160},{160,192},{192,224},{1,3... | collective-permute-start | bytes 392 | tf_op jit(solution)/shard_map/ppermute | solution.py:20
  41.8 5.3 %collective-permute-start.8 = (bf16[64,512]{1,0:T(8,128)(2,1)S(1)}, bf16[64,512]{1,0:T(8,128)(2,1)S(1)}, u32[]{:S(2)}, u32[]{:S(2)}) collective-permute-start(bf16[64,512]{1,0:T(8,128)(2,1)S(1)} %add_convert_fusion.6), channel_id=1, source_target_pairs={{0,32},{32,64},{64,96},{96,128},{128,160},{160,192},{192,224},{1,3... | collective-permute-start | bytes 196616 | tf_op jit(solution)/shard_map/ppermute | solution.py:20
  43.7 5.7 %collective-permute-start.4 = (bf16[64]{0:T(256)(128)(2,1)S(1)}, bf16[64]{0:T(256)(128)(2,1)S(1)}, u32[]{:S(2)}, u32[]{:S(2)}) collective-permute-start(bf16[64]{0:T(256)(128)(2,1)S(1)} %add_convert_fusion.10), channel_id=1, source_target_pairs={{0,32},{32,64},{64,96},{96,128},{128,160},{160,192},{192,224},{1,3... | collective-permute-start | bytes 392 | tf_op jit(solution)/shard_map/ppermute | solution.py:20
  47.2 4.7 %collective-permute-start.9 = (bf16[64,512]{1,0:T(8,128)(2,1)S(1)}, bf16[64,512]{1,0:T(8,128)(2,1)S(1)}, u32[]{:S(2)}, u32[]{:S(2)}) collective-permute-start(bf16[64,512]{1,0:T(8,128)(2,1)S(1)} %add_convert_fusion.5), channel_id=1, source_target_pairs={{0,32},{32,64},{64,96},{96,128},{128,160},{160,192},{192,224},{1,3... | collective-permute-start | bytes 196616 | tf_op jit(solution)/shard_map/ppermute | solution.py:20
  49.4 5.7 %collective-permute-start.5 = (bf16[64]{0:T(256)(128)(2,1)S(1)}, bf16[64]{0:T(256)(128)(2,1)S(1)}, u32[]{:S(2)}, u32[]{:S(2)}) collective-permute-start(bf16[64]{0:T(256)(128)(2,1)S(1)} %add_convert_fusion.9), channel_id=1, source_target_pairs={{0,32},{32,64},{64,96},{96,128},{128,160},{160,192},{192,224},{1,3... | collective-permute-start | bytes 392 | tf_op jit(solution)/shard_map/ppermute | solution.py:20
  52.0 6.1 %collective-permute-start.10 = (bf16[64,512]{1,0:T(8,128)(2,1)S(1)}, bf16[64,512]{1,0:T(8,128)(2,1)S(1)}, u32[]{:S(2)}, u32[]{:S(2)}) collective-permute-start(bf16[64,512]{1,0:T(8,128)(2,1)S(1)} %add_convert_fusion.4), channel_id=1, source_target_pairs={{0,32},{32,64},{64,96},{96,128},{128,160},{160,192},{192,224},{1,3... | collective-permute-start | bytes 196616 | tf_op jit(solution)/shard_map/ppermute | solution.py:20
  55.1 3.0 %collective-permute-start.6 = (bf16[64]{0:T(256)(128)(2,1)S(1)}, bf16[64]{0:T(256)(128)(2,1)S(1)}, u32[]{:S(2)}, u32[]{:S(2)}) collective-permute-start(bf16[64]{0:T(256)(128)(2,1)S(1)} %add_convert_fusion.8), channel_id=1, source_target_pairs={{0,32},{32,64},{64,96},{96,128},{128,160},{160,192},{192,224},{1,3... | collective-permute-start | bytes 392 | tf_op jit(solution)/shard_map/ppermute | solution.py:20
  58.2 5.1 %collective-permute-start.11 = (bf16[64,512]{1,0:T(8,128)(2,1)S(1)}, bf16[64,512]{1,0:T(8,128)(2,1)S(1)}, u32[]{:S(2)}, u32[]{:S(2)}) collective-permute-start(bf16[64,512]{1,0:T(8,128)(2,1)S(1)} %add_convert_fusion.3), channel_id=1, source_target_pairs={{0,32},{32,64},{64,96},{96,128},{128,160},{160,192},{192,224},{1,3... | collective-permute-start | bytes 196616 | tf_op jit(solution)/shard_map/ppermute | solution.py:20
  63.4 5.6 %collective-permute-start.12 = (bf16[64,512]{1,0:T(8,128)(2,1)S(1)}, bf16[64,512]{1,0:T(8,128)(2,1)S(1)}, u32[]{:S(2)}, u32[]{:S(2)}) collective-permute-start(bf16[64,512]{1,0:T(8,128)(2,1)S(1)} %add_convert_fusion.2), channel_id=1, source_target_pairs={{0,32},{32,64},{64,96},{96,128},{128,160},{160,192},{192,224},{1,3... | collective-permute-start | bytes 196616 | tf_op jit(solution)/shard_map/ppermute | solution.py:20
  69.1 5.6 %collective-permute-start.13 = (bf16[64,512]{1,0:T(8,128)(2,1)S(1)}, bf16[64,512]{1,0:T(8,128)(2,1)S(1)}, u32[]{:S(2)}, u32[]{:S(2)}) collective-permute-start(bf16[64,512]{1,0:T(8,128)(2,1)S(1)} %add_convert_fusion.1), channel_id=1, source_target_pairs={{0,32},{32,64},{64,96},{96,128},{128,160},{160,192},{192,224},{1,3... | collective-permute-start | bytes 196616 | tf_op jit(solution)/shard_map/ppermute | solution.py:20
  78.4 25.4 %all-to-all-start.1 = ((bf16[32,16,512]{2,1,0:T(8,128)(2,1)}), bf16[32,16,512]{2,1,0:T(8,128)(2,1)}, u32[]{:S(2)}, u32[]{:S(2)}) async-start(bf16[32,16,512]{2,1,0:T(8,128)(2,1)} %broadcast_select_fusion), calls=%async_computation.1 | async-start | bytes 1048576 | tf_op jit(solution)/shard_map/all_to_all | solution.py:111
  139.2 1.8 %copy-start.4 = (bf16[128,1024]{1,0:T(8,128)(2,1)S(1)}, bf16[128,1024]{1,0:T(8,128)(2,1)}, u32[]{:S(2)}) copy-start(bf16[128,1024]{1,0:T(8,128)(2,1)} %param.29) | copy-start | bytes 786436
  139.2 1.8 %copy-start.6 = (f32[128]{0:T(128)S(1)}, f32[128]{0:T(128)}, u32[]{:S(2)}) copy-start(f32[128]{0:T(128)} %param.25) | copy-start | bytes 1540
  139.2 1.8 %copy-start.7 = (f32[128]{0:T(128)S(1)}, f32[128]{0:T(128)}, u32[]{:S(2)}) copy-start(f32[128]{0:T(128)} %param.24) | copy-start | bytes 1540
  144.4 1.0 copy-start.3
  154.3 4.1 %copy-start.1 = (bf16[1024,1024]{1,0:T(8,128)(2,1)S(1)}, bf16[1024,1024]{1,0:T(8,128)(2,1)}, u32[]{:S(2)}) copy-start(bf16[1024,1024]{1,0:T(8,128)(2,1)} %param.30) | copy-start | bytes 6291460
  158.2 1.2 copy-start.2
where the time goes:
time: 163 us; the launch traced here: 160 us
  starting transfers between devices  66.7 us (41%)
  local copies, waits for them, and re-layouts  38.3 us (23%)
  matrix products  20 us (12%)
  other arithmetic  18.8 us (12%)
  waiting for transfers between devices  15.5 us (10%)
    ppermute x14, starting transfers between devices, from_behind(): lax.ppermute(value, axis, [(source, source + steps) for source in range(l...  45.9 us
    gather x2, local copies, waits for them, and re-layouts, local(): jnp.take(received.reshape(-1, 2 * width), neighbour_slot.reshape(-1), axi...  22.3 us
    all_to_all x1, waiting for transfers between devices, local(): lax.all_to_all(outgoing, 'node', split_axis=0, concat_axis=0, tiled=True)  11.1 us
    all_to_all x1, starting transfers between devices, local(): lax.all_to_all(request_rows, 'node', split_axis=0, concat_axis=0, tiled=T...  11 us
    all_to_all x1, starting transfers between devices, local(): lax.all_to_all(outgoing, 'node', split_axis=0, concat_axis=0, tiled=True)  9.81 us
    select_n x2, other arithmetic, local(): jnp.take(received.reshape(-1, 2 * width), neighbour_slot.reshape(-1), axi...  9.51 us
    unnamed x23, local copies, waits for them, and re-layouts  7.91 us
    ppermute x14, waiting for transfers between devices, from_behind(): lax.ppermute(value, axis, [(source, source + steps) for source in range(l...  4.36 us
  transfers between devices with their start and end apart: 16, of which 6 were waited for; matrix products, arithmetic and copies ran while one was open for 7% of the time, Pallas kernels for 0%

commit v1 on v0

v1 whole, which is shorter than its diff:
```python
import functools
import math

import jax
import jax.numpy as jnp
from jax import lax
from jax.experimental import pallas as pl
from jax.experimental.pallas import tpu as pltpu
from jax.sharding import PartitionSpec as P

MESH = pl.DeviceIdType.MESH
HEADS = 8
F32, BF16 = jnp.float32, jnp.bfloat16
EXACT = lax.Precision.HIGHEST
SINE = (0.5, -0.020833322778344154, 0.0002604078035801649, -1.5475785630769678e-06, 5.088033105948853e-09)
TURN_HIGH = 6.28125
TURN_LOW = 2.0 * math.pi - TURN_HIGH
ROUNDER = 12582912.0


def cosine(angle):
    turns = (angle * (0.5 / math.pi) + ROUNDER) - ROUNDER
    rest = (angle - turns * TURN_HIGH) - turns * TURN_LOW
    square = rest * rest
    poly = SINE[4]
    for term in SINE[3::-1]:
        poly = poly * square + term
    half = rest * poly
    return 1.0 - 2.0 * (half * half)


def nn(a, b, precision=None):
    return lax.dot_general(a, b, (((1,), (0,)), ((), ())), precision=precision, preferred_element_type=F32)


def nt(a, b, precision=None):
    return lax.dot_general(a, b, (((1,), (1,)), ((), ())), precision=precision, preferred_element_type=F32)


def tn(a, b):
    return lax.dot_general(a, b, (((0,), (0,)), ((), ())), preferred_element_type=F32)


def kernel(
    lanes, nodes,
    source_ref, bucket_ref, slot_ref, age_ref, count_ref, request_ref, start_ref,
    decay_ref, frequency_ref, phase_ref, message_hbm, query_hbm, keyval_hbm, time_hbm, output_hbm, skip_hbm,
    embedding_ref, memory_ref,
    wm, wq, wkv, wt, wo, ws, weight_sem,
    lane_source, lane_bucket, asked_out, asked_in, send_buf, far,
    summed, touched, enc, slots, timed, acc, scores, table_own, value, score, mix, qk,
    lane_send, lane_recv, ask_send, ask_recv, row_send, row_recv,
):
    lane, node = lax.axis_index("lane"), lax.axis_index("node")
    owned, channels = start_ref.shape
    events, neighbours = slot_ref.shape
    cap = request_ref.shape[1]
    width = wq.shape[1]
    size = width // HEADS
    total = nodes * cap

    loads = [
        pltpu.make_async_copy(source, target, weight_sem.at[i])
        for i, (source, target) in enumerate(
            ((message_hbm, wm), (query_hbm, wq), (keyval_hbm, wkv), (time_hbm, wt), (skip_hbm, ws), (output_hbm, wo))
        )
    ]
    for load in loads:
        load.start()

    barrier = pltpu.get_barrier_semaphore()

    def greet_lane(k, _):
        pl.semaphore_signal(barrier, inc=1, device_id=(lax.rem(lane + k, lanes), node), device_id_type=MESH)
        return 0

    def greet_node(k, _):
        pl.semaphore_signal(barrier, inc=1, device_id=(lane, lax.rem(node + k, nodes)), device_id_type=MESH)
        return 0

    lax.fori_loop(1, lanes, greet_lane, 0)
    lax.fori_loop(1, nodes, greet_node, 0)

    for o in range(nodes):
        asked_out[o, :, 0:cap] = request_ref[o : o + 1, :]
    asked_in[pl.ds(node, 1), :, 0:cap] = asked_out[pl.ds(node, 1), :, 0:cap]
    lane_source[pl.ds(lane, 1)] = source_ref[...][None]
    lane_bucket[pl.ds(lane, 1)] = bucket_ref[...][None]
    te = frequency_ref.shape[1]
    frequency = jnp.broadcast_to(frequency_ref[...], (te, te)).T
    phase = jnp.broadcast_to(phase_ref[...], (te, te)).T
    slots[0:neighbours, :] = slot_ref[...].T
    ages = age_ref[...].T.astype(F32)
    for j in range(neighbours):
        enc[j] = cosine(frequency * ages[j : j + 1, :] + phase)
    node_row = lax.broadcasted_iota(jnp.int32, (owned, events), 0)
    own_member = (node_row == source_ref[...]).astype(F32)
    picker = own_member.T.astype(BF16)

    pl.semaphore_wait(barrier, lanes - 1 + nodes - 1)

    def lane_copies(k):
        to = lax.rem(lane + k, lanes)
        return [
            pltpu.make_async_remote_copy(
                src_ref=ref, dst_ref=held.at[lane], send_sem=lane_send.at[i, k], recv_sem=lane_recv.at[i, k],
                device_id=(to, node), device_id_type=MESH,
            )
            for i, (ref, held) in enumerate(((source_ref, lane_source), (bucket_ref, lane_bucket)))
        ]

    def ask_copy(k):
        to = lax.rem(node + k, nodes)
        return pltpu.make_async_remote_copy(
            src_ref=asked_out.at[to], dst_ref=asked_in.at[node], send_sem=ask_send.at[k], recv_sem=ask_recv.at[k],
            device_id=(lane, to), device_id_type=MESH,
        )

    def row_copy(k):
        to = lax.rem(node + k, nodes)
        return pltpu.make_async_remote_copy(
            src_ref=send_buf.at[to], dst_ref=far.at[node], send_sem=row_send.at[k], recv_sem=row_recv.at[k],
            device_id=(lane, to), device_id_type=MESH,
        )

    def loop(count, body):
        def step(k, _):
            body(k)
            return 0

        lax.fori_loop(1, count, step, 0)

    loop(lanes, lambda k: [copy.start() for copy in lane_copies(k)])
    loop(nodes, lambda k: ask_copy(k).start())
    loop(lanes, lambda k: [copy.wait() for copy in lane_copies(k)])

    loads[0].wait()
    ones = jnp.ones((te, events), BF16)
    sums = []
    for l in range(lanes):
        member = (node_row == lane_source[l]).astype(F32)
        encoded = cosine(frequency * lane_bucket[l].astype(F32) + phase)
        sums.append(nt(member, encoded, EXACT))
        touched[l] = nt(member.astype(BF16), ones)
    summed[...] = nn(jnp.concatenate(sums, axis=0), wm[...], EXACT).reshape(lanes, owned, channels)
    decay = -decay_ref[...]
    state = start_ref[...]

    def after(state, count, added):
        return jnp.exp(decay * jnp.concatenate([count] * (channels // te), axis=1)) * state + added

    for l in range(lanes - 1):
        state = jnp.where(l < lane, after(state, touched[l], summed[l]), state)
    memory_ref[...] = after(state, touched[pl.ds(lane, 1)][0], summed[pl.ds(lane, 1)][0])
    rows = state.astype(BF16)
    table_own[...] = rows

    loop(nodes, lambda k: ask_copy(k).wait())
    asked = jnp.concatenate([asked_in[o, :, :] for o in range(nodes)], axis=0).T
    node_lane = lax.broadcasted_iota(jnp.int32, (cap, owned), 1)
    picks = jnp.concatenate([(asked[0:cap, o : o + 1] == node_lane).astype(F32) for o in range(nodes)], axis=0)
    send_buf[...] = nn(picks.astype(BF16), rows).astype(BF16).reshape(nodes, cap, channels)
    loop(nodes, lambda k: row_copy(k).start())
    far[pl.ds(node, 1)] = send_buf[pl.ds(node, 1)]

    for load in loads[1:]:
        load.wait()
    query = nn(picker, nn(rows, wq[...]).astype(BF16)).astype(BF16)
    query_in = nn(picker, rows).astype(BF16)
    timed[...] = jnp.zeros_like(timed)
    for h in range(HEADS):
        head = query[:, h * size : (h + 1) * size]
        qk[h * events : (h + 1) * events, :] = nt(head, wkv[:, h * size : (h + 1) * size]).astype(BF16)
        spread = nt(wt[:, h * size : (h + 1) * size], head)
        for j in range(neighbours):
            timed[h, j : j + 1, :] = jnp.sum(spread * enc[j], axis=0, keepdims=True)
    value[total : total + owned, :] = nn(rows, wkv[:, width:]).astype(BF16)
    own_score = nt(rows, qk[...])
    scores[...] = jnp.zeros_like(scores)
    for h in range(HEADS):
        scores[h, neighbours : neighbours + 1, :] = jnp.sum(
            own_member * own_score[:, h * events : (h + 1) * events], axis=0, keepdims=True
        )
    acc[...] = jnp.zeros_like(acc)

    loop(nodes, lambda k: row_copy(k).wait())
    table = far[...].reshape(total, channels)
    value[0:total, :] = nn(table, wkv[:, width:]).astype(BF16)
    score[...] = nt(table, qk[...])

    piece = 32
    piece_row = lax.broadcasted_iota(jnp.int32, (piece, events), 0)

    def gather(c, _):
        base = pl.multiple_of(c * piece, piece)
        for j in range(neighbours):
            hit = (piece_row + base) == slots[j : j + 1, :]
            for h in range(HEADS):
                found = jnp.where(hit, score[pl.ds(base, piece), h * events : (h + 1) * events], 0.0)
                acc[h, j] += jnp.sum(found.reshape(piece // 8, 8, events), axis=0)
        return 0

    lax.fori_loop(0, total // piece, gather, 0)
    for h in range(HEADS):
        for j in range(neighbours):
            scores[h, j : j + 1, :] = jnp.sum(acc[h, j], axis=0, keepdims=True)
    logits = (scores[...] + timed[...]) * (1.0 / math.sqrt(size))
    place = lax.broadcasted_iota(jnp.int32, logits.shape, 1)
    valid = (place < count_ref[...][None]) | (place == neighbours)
    logits = jnp.where(valid, logits, -1e30)
    expo = jnp.where(valid, jnp.exp(logits - jnp.max(logits, axis=1, keepdims=True)), 0.0)
    scores[...] = (expo / jnp.sum(expo, axis=1, keepdims=True)).astype(BF16).astype(F32)

    def scatter(c, _):
        base = pl.multiple_of(c * piece, piece)
        hits = [(piece_row + base) == slots[j : j + 1, :] for j in range(neighbours)]
        for h in range(HEADS):
            put = jnp.zeros((piece, events), F32)
            for j in range(neighbours):
                put += jnp.where(hits[j], scores[h, j : j + 1, :], 0.0)
            mix[pl.ds(base, piece), h * events : (h + 1) * events] = put.astype(BF16)
        return 0

    lax.fori_loop(0, total // piece, scatter, 0)
    attended = []
    for h in range(HEADS):
        mix[total : total + owned, h * events : (h + 1) * events] = (
            own_member * scores[h, neighbours : neighbours + 1, :]
        ).astype(BF16)
        attended.append(tn(mix[:, h * events : (h + 1) * events], value[:, h * size : (h + 1) * size]).astype(BF16))
    embedding_ref[...] = (nn(jnp.concatenate(attended, axis=1), wo[...]) + nn(query_in, ws[...])).astype(BF16)


def local(
    source_row, time_bucket, neighbour_slot, neighbour_age, neighbour_count, request_rows, memory_start, decay_rate,
    time_frequency, time_phase, weight_message, weight_query, weight_keyval, weight_time, weight_output, weight_skip,
):
    lanes, nodes = lax.axis_size("lane"), lax.axis_size("node")
    owned, channels = memory_start.shape
    events, neighbours = neighbour_slot.shape
    cap = request_rows.shape[1]
    te, width = weight_time.shape
    total = nodes * cap
    row = lambda x: x.reshape(1, -1)
    vmem = pl.BlockSpec(memory_space=pltpu.VMEM)
    hbm = pl.BlockSpec(memory_space=pl.ANY)
    dma = pltpu.SemaphoreType.DMA
    embedding, memory = pl.pallas_call(
        functools.partial(kernel, lanes, nodes),
        out_shape=(
            jax.ShapeDtypeStruct((events, width), BF16),
            jax.ShapeDtypeStruct((owned, channels), F32),
        ),
        in_specs=[vmem] * 10 + [hbm] * 6,
        out_specs=(vmem, vmem),
        scratch_shapes=[
            pltpu.VMEM(weight_message.shape, F32),
            pltpu.VMEM(weight_query.shape, BF16),
            pltpu.VMEM(weight_keyval.shape, BF16),
            pltpu.VMEM(weight_time.shape, BF16),
            pltpu.VMEM(weight_output.shape, BF16),
            pltpu.VMEM(weight_skip.shape, BF16),
            dma((6,)),
            pltpu.VMEM((lanes, 1, events), jnp.int32),
            pltpu.VMEM((lanes, 1, events), jnp.int32),
            pltpu.VMEM((nodes, 1, 128), jnp.int32),
            pltpu.VMEM((nodes, 1, 128), jnp.int32),
            pltpu.VMEM((nodes, cap, channels), BF16),
            pltpu.VMEM((nodes, cap, channels), BF16),
            pltpu.VMEM((lanes, owned, channels), F32),
            pltpu.VMEM((lanes, owned, te), F32),
            pltpu.VMEM((neighbours, te, events), F32),
            pltpu.VMEM((16, events), jnp.int32),
            pltpu.VMEM((HEADS, 16, events), F32),
            pltpu.VMEM((HEADS, neighbours, 8, events), F32),
            pltpu.VMEM((HEADS, 16, events), F32),
            pltpu.VMEM((owned, channels), BF16),
            pltpu.VMEM((total + owned, width), BF16),
            pltpu.VMEM((total, HEADS * events), F32),
            pltpu.VMEM((total + owned, HEADS * events), BF16),
            pltpu.VMEM((HEADS * events, channels), BF16),
            dma((2, lanes)),
            dma((2, lanes)),
            dma((nodes,)),
            dma((nodes,)),
            dma((nodes,)),
            dma((nodes,)),
        ],
        compiler_params=pltpu.CompilerParams(collective_id=0, has_side_effects=True),
    )(
        row(source_row), row(time_bucket), neighbour_slot, neighbour_age, row(neighbour_count), request_rows,
        memory_start, row(decay_rate), row(time_frequency), row(time_phase), weight_message, weight_query,
        weight_keyval, weight_time, weight_output, weight_skip,
    )
    return embedding, memory[None]


def solution(mesh):
    both, rows = P(("lane", "node")), P(("lane", "node"), None)
    return jax.shard_map(
        local,
        mesh=mesh,
        in_specs=(both, both, rows, rows, both, rows, P("node", None)) + (P(),) * 9,
        out_specs=(rows, P("lane", "node", None)),
        check_vma=False,
    )
```

time: 163 us -> 48 us (0.29); the launches traced: 160 us -> 47.7 us
  starting transfers between devices: 66.7 us -> 0 us
  Pallas kernels: 0 us -> 39.6 us
  local copies, waits for them, and re-layouts: 38.3 us -> 7.46 us
  matrix products: 20 us -> 0 us
  other arithmetic: 18.8 us -> 0 us
  waiting for transfers between devices: 15.5 us -> 0 us
    ppermute x14 -> x0, starting transfers between devices: 45.9 us -> none  [from_behind(): lax.ppermute(value, axis, [(source, source + steps) for source in range(l...]
    pallas_call x0 -> x1, Pallas kernels: none -> 39.6 us  [local(): pl.pallas_call(functools.partial(kernel, lanes, nodes), out_shape=(jax.Sh...]
    gather x4 -> x0, local copies, waits for them, and re-layouts: 25.2 us -> none  [the longest x2 22.3 us: local(): jnp.take(received.reshape(-1, 2 * width), neighbour_slot.reshape(-1), axi...]
    all_to_all x2 -> x0, starting transfers between devices: 20.8 us -> none  [the longest x1 11 us: local(): lax.all_to_all(request_rows, 'node', split_axis=0, concat_axis=0, tiled=T...]
    dot_general x10 -> x0, matrix products: 20 us -> none  [the longest x1 3.87 us: attend(): jnp.einsum('ehk,ekhd->ehd', weights, value_heads, preferred_element_type=...]
    select_n x5 -> x0, other arithmetic: 11.1 us -> none  [the longest x2 9.51 us: local(): jnp.take(received.reshape(-1, 2 * width), neighbour_slot.reshape(-1), axi...]
    all_to_all x2 -> x0, waiting for transfers between devices: 11.1 us -> none  [the longest x1 11.1 us: local(): lax.all_to_all(outgoing, 'node', split_axis=0, concat_axis=0, tiled=True)]
    ppermute x14 -> x0, waiting for transfers between devices: 4.36 us -> none  [from_behind(): lax.ppermute(value, axis, [(source, source + steps) for source in range(l...]
  transfers between devices with their start and end apart: 16 -> 0, of which waited for: 6 -> 0; matrix products, arithmetic and copies ran while one was open for 7% -> 0% of each run, Pallas kernels for 0% -> 0%
where the time goes in v1:
time: 48 us; the launch traced here: 47.7 us
  Pallas kernels  39.6 us (82%)
  local copies, waits for them, and re-layouts  7.46 us (16%)
  between operations  0.64 us (1%)
    pallas_call x1, Pallas kernels, local(): pl.pallas_call(functools.partial(kernel, lanes, nodes), out_shape=(jax.Sh...  39.6 us
    unnamed x5, local copies, waits for them, and re-layouts  7.46 us

profile of v1, /device:TPU:1, one launch (start us, length us, event | category | flops | bytes accessed | tf_op | source)
XLA Modules:
  0.0 47.7 jit_solution(15163634781794909898)
XLA Ops:
  0.6 1.4 %copy.20.request_ref = s32[32,16]{1,0:T(8,128)} copy(s32[32,16]{0,1:T(8,128)} %param.21) | data formatting | bytes 4096 | tf_op args[5]
  2.0 1.4 %copy.18.slot_ref = s32[128,10]{1,0:T(8,128)} copy(s32[128,10]{0,1:T(8,128)} %param.18) | data formatting | bytes 10240 | tf_op args[2]
  3.4 1.4 %copy.19.age_ref = s32[128,10]{1,0:T(8,128)} copy(s32[128,10]{0,1:T(8,128)} %param.19) | data formatting | bytes 10240 | tf_op args[3]
  4.9 39.6 %shard_map.167 = (bf16[128,1024]{1,0:T(8,128)(2,1)}, f32[64,512]{1,0:T(8,128)}) custom-call(s32[1,128]{1,0:T(1,128)} %bitcast.9, s32[1,128]{1,0:T(1,128)} %bitcast.10, s32[128,10]{1,0:T(8,128)} %copy.18.slot_ref, s32[128,10]{1,0:T(8,128)} %copy.19.age_ref, s32[1,128]{1,0:T(1,128)} %bitcast.11, s32[32,16]{1,0:T(8,128)} %copy.20.request_ref, ...), custom_call_target="tpu_custom_call" | custom-call | tf_op jit(solution)/shard_map/pallas_call | solution.py:248
  44.5 1.7 %copy.23 = bf16[128,1024]{1,0:T(8,128)(2,1)} copy(bf16[128,1024]{1,0:T(8,128)(2,1)} %get-tuple-element.8) | data formatting | bytes 524288
  46.2 1.6 %copy.24 = f32[1,64,512]{2,1,0:T(8,128)} copy(f32[1,64,512]{2,1,0:T(8,128)} %bitcast.7) | data formatting | bytes 262144

commit v2 on v1

--- a/solution.py
+++ b/solution.py
@@ -43,28 +43,32 @@
 
 def kernel(
     lanes, nodes,
-    source_ref, bucket_ref, slot_ref, age_ref, count_ref, request_ref, start_ref,
-    decay_ref, frequency_ref, phase_ref, message_hbm, query_hbm, keyval_hbm, time_hbm, output_hbm, skip_hbm,
-    embedding_ref, memory_ref,
-    wm, wq, wkv, wt, wo, ws, weight_sem,
+    source_hbm, bucket_hbm, request_hbm, frequency_hbm, phase_hbm, age_hbm, slot_hbm, count_hbm, decay_hbm, start_hbm,
+    message_hbm, query_hbm, keyval_hbm, time_hbm, skip_hbm,
+    attended_ref, base_ref, memory_ref,
+    source_ref, bucket_ref, request_ref, frequency_ref, phase_ref, age_ref, slot_ref, count_ref, decay_ref, start_ref,
+    wm, wq, wkv, wt, ws, load_sem,
     lane_source, lane_bucket, asked_out, asked_in, send_buf, far,
-    summed, touched, enc, slots, timed, acc, scores, table_own, value, score, mix, qk,
+    summed, touched, enc, timed, acc, scores, table_own, value, score, mix, qk,
     lane_send, lane_recv, ask_send, ask_recv, row_send, row_recv,
 ):
     lane, node = lax.axis_index("lane"), lax.axis_index("node")
     owned, channels = start_ref.shape
-    events, neighbours = slot_ref.shape
-    cap = request_ref.shape[1]
+    neighbours, events = slot_ref.shape
+    cap = request_ref.shape[0]
     width = wq.shape[1]
     size = width // HEADS
     total = nodes * cap
 
-    loads = [
-        pltpu.make_async_copy(source, target, weight_sem.at[i])
-        for i, (source, target) in enumerate(
-            ((message_hbm, wm), (query_hbm, wq), (keyval_hbm, wkv), (time_hbm, wt), (skip_hbm, ws), (output_hbm, wo))
-        )
-    ]
+    sources = (
+        source_hbm, bucket_hbm, request_hbm, frequency_hbm, phase_hbm, age_hbm, slot_hbm, count_hbm, decay_hbm,
+        start_hbm, message_hbm, query_hbm, keyval_hbm, time_hbm, skip_hbm,
+    )
+    held = (
+        source_ref, bucket_ref, request_ref, frequency_ref, phase_ref, age_ref, slot_ref, count_ref, decay_ref,
+        start_ref, wm, wq, wkv, wt, ws,
+    )
+    loads = [pltpu.make_async_copy(a, b, load_sem.at[i]) for i, (a, b) in enumerate(zip(sources, held))]
     for load in loads:
         load.start()
 
@@ -81,16 +85,18 @@
     lax.fori_loop(1, lanes, greet_lane, 0)
     lax.fori_loop(1, nodes, greet_node, 0)
 
+    for load in loads[:6]:
+        load.wait()
+    requests = request_ref[...].T
     for o in range(nodes):
-        asked_out[o, :, 0:cap] = request_ref[o : o + 1, :]
+        asked_out[o, :, 0:cap] = requests[o : o + 1, :]
     asked_in[pl.ds(node, 1), :, 0:cap] = asked_out[pl.ds(node, 1), :, 0:cap]
     lane_source[pl.ds(lane, 1)] = source_ref[...][None]
     lane_bucket[pl.ds(lane, 1)] = bucket_ref[...][None]
     te = frequency_ref.shape[1]
     frequency = jnp.broadcast_to(frequency_ref[...], (te, te)).T
     phase = jnp.broadcast_to(phase_ref[...], (te, te)).T
-    slots[0:neighbours, :] = slot_ref[...].T
-    ages = age_ref[...].T.astype(F32)
+    ages = age_ref[...].astype(F32)
     for j in range(neighbours):
         enc[j] = cosine(frequency * ages[j : j + 1, :] + phase)
     node_row = lax.broadcasted_iota(jnp.int32, (owned, events), 0)
@@ -134,7 +140,8 @@
     loop(nodes, lambda k: ask_copy(k).start())
     loop(lanes, lambda k: [copy.wait() for copy in lane_copies(k)])
 
-    loads[0].wait()
+    for load in loads[6:11]:
+        load.wait()
     ones = jnp.ones((te, events), BF16)
     sums = []
     for l in range(lanes):
@@ -163,10 +170,10 @@
     loop(nodes, lambda k: row_copy(k).start())
     far[pl.ds(node, 1)] = send_buf[pl.ds(node, 1)]
 
-    for load in loads[1:]:
+    for load in loads[11:]:
         load.wait()
     query = nn(picker, nn(rows, wq[...]).astype(BF16)).astype(BF16)
-    query_in = nn(picker, rows).astype(BF16)
+    base_ref[...] = nn(nn(picker, rows).astype(BF16), ws[...])
     timed[...] = jnp.zeros_like(timed)
     for h in range(HEADS):
         head = query[:, h * size : (h + 1) * size]
@@ -194,7 +201,7 @@
     def gather(c, _):
         base = pl.multiple_of(c * piece, piece)
         for j in range(neighbours):
-            hit = (piece_row + base) == slots[j : j + 1, :]
+            hit = (piece_row + base) == slot_ref[j : j + 1, :]
             for h in range(HEADS):
                 found = jnp.where(hit, score[pl.ds(base, piece), h * events : (h + 1) * events], 0.0)
                 acc[h, j] += jnp.sum(found.reshape(piece // 8, 8, events), axis=0)
@@ -213,7 +220,7 @@
 
     def scatter(c, _):
         base = pl.multiple_of(c * piece, piece)
-        hits = [(piece_row + base) == slots[j : j + 1, :] for j in range(neighbours)]
+        hits = [(piece_row + base) == slot_ref[j : j + 1, :] for j in range(neighbours)]
         for h in range(HEADS):
             put = jnp.zeros((piece, events), F32)
             for j in range(neighbours):
@@ -222,13 +229,36 @@
         return 0
 
     lax.fori_loop(0, total // piece, scatter, 0)
-    attended = []
     for h in range(HEADS):
         mix[total : total + owned, h * events : (h + 1) * events] = (
             own_member * scores[h, neighbours : neighbours + 1, :]
         ).astype(BF16)
-        attended.append(tn(mix[:, h * events : (h + 1) * events], value[:, h * size : (h + 1) * size]).astype(BF16))
-    embedding_ref[...] = (nn(jnp.concatenate(attended, axis=1), wo[...]) + nn(query_in, ws[...])).astype(BF16)
+        attended_ref[:, h * size : (h + 1) * size] = tn(
+            mix[:, h * events : (h + 1) * events], value[:, h * size : (h + 1) * size]
+        ).astype(BF16)
+
+
+def finish(
+    attended_hbm, base_hbm, memory_hbm, output_hbm, embedding_ref, lane_memory_ref, attended_ref, base_ref, output_ref, sem
+):
+    half = output_ref.shape[0] // 2
+    loads = [
+        pltpu.make_async_copy(a, b, sem.at[i])
+        for i, (a, b) in enumerate(
+            (
+                (attended_hbm, attended_ref), (output_hbm.at[0:half], output_ref.at[0:half]), (base_hbm, base_ref),
+                (output_hbm.at[half:], output_ref.at[half:]), (memory_hbm, lane_memory_ref),
+            )
+        )
+    ]
+    for load in loads:
+        load.start()
+    for load in loads[0:3]:
+        load.wait()
+    part = nn(attended_ref[:, 0:half], output_ref[0:half, :]) + base_ref[...]
+    loads[3].wait()
+    embedding_ref[...] = (nn(attended_ref[:, half:], output_ref[half:, :]) + part).astype(BF16)
+    loads[4].wait()
 
 
 def local(
@@ -243,24 +273,34 @@
     total = nodes * cap
     row = lambda x: x.reshape(1, -1)
     vmem = pl.BlockSpec(memory_space=pltpu.VMEM)
-    hbm = pl.BlockSpec(memory_space=pl.ANY)
+    hbm = pl.BlockSpec(memory_space=pltpu.HBM)
     dma = pltpu.SemaphoreType.DMA
-    embedding, memory = pl.pallas_call(
+    attended, base, memory = pl.pallas_call(
         functools.partial(kernel, lanes, nodes),
         out_shape=(
             jax.ShapeDtypeStruct((events, width), BF16),
+            jax.ShapeDtypeStruct((events, width), F32),
             jax.ShapeDtypeStruct((owned, channels), F32),
         ),
-        in_specs=[vmem] * 10 + [hbm] * 6,
-        out_specs=(vmem, vmem),
+        in_specs=[hbm] * 15,
+        out_specs=(vmem, vmem, vmem),
         scratch_shapes=[
+            pltpu.VMEM((1, events), jnp.int32),
+            pltpu.VMEM((1, events), jnp.int32),
+            pltpu.VMEM((cap, nodes), jnp.int32),
+            pltpu.VMEM((1, te), F32),
+            pltpu.VMEM((1, te), F32),
+            pltpu.VMEM((neighbours, events), jnp.int32),
+            pltpu.VMEM((neighbours, events), jnp.int32),
+            pltpu.VMEM((1, events), jnp.int32),
+            pltpu.VMEM((1, channels), F32),
+            pltpu.VMEM((owned, channels), F32),
             pltpu.VMEM(weight_message.shape, F32),
             pltpu.VMEM(weight_query.shape, BF16),
             pltpu.VMEM(weight_keyval.shape, BF16),
             pltpu.VMEM(weight_time.shape, BF16),
-            pltpu.VMEM(weight_output.shape, BF16),
             pltpu.VMEM(weight_skip.shape, BF16),
-            dma((6,)),
+            dma((15,)),
             pltpu.VMEM((lanes, 1, events), jnp.int32),
             pltpu.VMEM((lanes, 1, events), jnp.int32),
             pltpu.VMEM((nodes, 1, 128), jnp.int32),
@@ -270,7 +310,6 @@
             pltpu.VMEM((lanes, owned, channels), F32),
             pltpu.VMEM((lanes, owned, te), F32),
             pltpu.VMEM((neighbours, te, events), F32),
-            pltpu.VMEM((16, events), jnp.int32),
             pltpu.VMEM((HEADS, 16, events), F32),
             pltpu.VMEM((HEADS, neighbours, 8, events), F32),
             pltpu.VMEM((HEADS, 16, events), F32),
@@ -286,12 +325,30 @@
             dma((nodes,)),
             dma((nodes,)),
         ],
-        compiler_params=pltpu.CompilerParams(collective_id=0, has_side_effects=True),
+        compiler_params=pltpu.CompilerParams(
+            collective_id=0, has_side_effects=True, vmem_limit_bytes=56 * 1024 * 1024
+        ),
     )(
-        row(source_row), row(time_bucket), neighbour_slot, neighbour_age, row(neighbour_count), request_rows,
-        memory_start, row(decay_rate), row(time_frequency), row(time_phase), weight_message, weight_query,
-        weight_keyval, weight_time, weight_output, weight_skip,
+        row(source_row), row(time_bucket), request_rows.T, row(time_frequency), row(time_phase), neighbour_age.T,
+        neighbour_slot.T, row(neighbour_count), row(decay_rate), memory_start, weight_message, weight_query,
+        weight_keyval, weight_time, weight_skip,
     )
+    embedding, memory = pl.pallas_call(
+        finish,
+        out_shape=(
+            jax.ShapeDtypeStruct((events, width), BF16),
+            jax.ShapeDtypeStruct((owned, channels), F32),
+        ),
+        in_specs=[hbm] * 4,
+        out_specs=(vmem, vmem),
+        scratch_shapes=[
+            pltpu.VMEM((events, width), BF16),
+            pltpu.VMEM((events, width), F32),
+            pltpu.VMEM(weight_output.shape, BF16),
+            dma((5,)),
+        ],
+        compiler_params=pltpu.CompilerParams(vmem_limit_bytes=56 * 1024 * 1024),
+    )(attended, base, memory, weight_output)
     return embedding, memory[None]
 
 

time: 48 us -> 42.1 us (0.88)
  local copies, waits for them, and re-layouts: 7.46 us -> 0 us
  Pallas kernels: 39.6 us -> 41.4 us
    unnamed x5 -> x0, local copies, waits for them, and re-layouts: 7.46 us -> none
    pallas_call x0 -> x1, Pallas kernels: none -> 2.89 us  [local(): pl.pallas_call(finish, out_shape=(jax.ShapeDtypeStruct((events, width), B...]
    pallas_call x1, Pallas kernels: 39.6 us -> 38.5 us  [local(): pl.pallas_call(functools.partial(kernel, lanes, nodes), out_shape=(jax.Sh...]
where the time goes in v2:
time: 42.1 us; the launch traced here: 42 us
  Pallas kernels  41.4 us (98%)
  between operations  0.64 us (2%)
    pallas_call x1, Pallas kernels, local(): pl.pallas_call(functools.partial(kernel, lanes, nodes), out_shape=(jax.Sh...  38.5 us
    pallas_call x1, Pallas kernels, local(): pl.pallas_call(finish, out_shape=(jax.ShapeDtypeStruct((events, width), B...  2.89 us

profile of v2, /device:TPU:1, one launch (start us, length us, event | category | flops | bytes accessed | tf_op | source)
XLA Modules:
  0.0 42.0 jit_solution(9722702292317005824)
XLA Ops:
  0.6 38.5 %shard_map.167 = (bf16[128,1024]{1,0:T(8,128)(2,1)}, f32[128,1024]{1,0:T(8,128)}, f32[64,512]{1,0:T(8,128)}) custom-call(s32[1,128]{1,0:T(1,128)} %bitcast.14, s32[1,128]{1,0:T(1,128)} %bitcast.15, s32[16,32]{1,0:T(8,128)} %bitcast.10, f32[1,128]{1,0:T(1,128)} %bitcast.16, f32[1,128]{1,0:T(1,128)} %bitcast.17, s32[10,128]{1,0:T(8,128)} %bitcast.11, ...), custom_call_target="tpu_custom_call" | custom-call | tf_op jit(solution)/shard_map/pallas_call | solution.py:278
  39.1 2.9 %shard_map.168 = (bf16[128,1024]{1,0:T(8,128)(2,1)}, f32[64,512]{1,0:T(8,128)}) custom-call(bf16[128,1024]{1,0:T(8,128)(2,1)} %get-tuple-element.7.attended_hbm, f32[128,1024]{1,0:T(8,128)} %get-tuple-element.8.base_hbm, f32[64,512]{1,0:T(8,128)} %get-tuple-element.9.memory_hbm, bf16[1024,1024]{1,0:T(8,128)(2,1)} %output_hbm.1), custom_call_target="tpu_custom_call" | custom-call | tf_op jit(solution)/shard_map/pallas_call | solution.py:336

commit v3 on v2

--- a/solution.py
+++ b/solution.py
@@ -10,6 +10,7 @@
 
 MESH = pl.DeviceIdType.MESH
 HEADS = 8
+RING = 8
 F32, BF16 = jnp.float32, jnp.bfloat16
 EXACT = lax.Precision.HIGHEST
 SINE = (0.5, -0.020833322778344154, 0.0002604078035801649, -1.5475785630769678e-06, 5.088033105948853e-09)
@@ -46,11 +47,11 @@
     source_hbm, bucket_hbm, request_hbm, frequency_hbm, phase_hbm, age_hbm, slot_hbm, count_hbm, decay_hbm, start_hbm,
     message_hbm, query_hbm, keyval_hbm, time_hbm, skip_hbm,
     attended_ref, base_ref, memory_ref,
-    source_ref, bucket_ref, request_ref, frequency_ref, phase_ref, age_ref, slot_ref, count_ref, decay_ref, start_ref,
+    event_ref, request_ref, frequency_ref, phase_ref, age_ref, slot_ref, count_ref, decay_ref, start_ref,
     wm, wq, wkv, wt, ws, load_sem,
-    lane_source, lane_bucket, asked_out, asked_in, send_buf, far,
+    lane_event, asked_out, asked_in, send_buf, far,
     summed, touched, enc, timed, acc, scores, table_own, value, score, mix, qk,
-    lane_send, lane_recv, ask_send, ask_recv, row_send, row_recv,
+    lane_send, lane_recv, ask_send, ask_recv, row_send, row_recv, met,
 ):
     lane, node = lax.axis_index("lane"), lax.axis_index("node")
     owned, channels = start_ref.shape
@@ -59,31 +60,44 @@
     width = wq.shape[1]
     size = width // HEADS
     total = nodes * cap
+    shift = cap.bit_length() - 1
 
     sources = (
         source_hbm, bucket_hbm, request_hbm, frequency_hbm, phase_hbm, age_hbm, slot_hbm, count_hbm, decay_hbm,
         start_hbm, message_hbm, query_hbm, keyval_hbm, time_hbm, skip_hbm,
     )
     held = (
-        source_ref, bucket_ref, request_ref, frequency_ref, phase_ref, age_ref, slot_ref, count_ref, decay_ref,
+        event_ref.at[0:1], event_ref.at[1:2], request_ref, frequency_ref, phase_ref, age_ref, slot_ref, count_ref, decay_ref,
         start_ref, wm, wq, wkv, wt, ws,
     )
     loads = [pltpu.make_async_copy(a, b, load_sem.at[i]) for i, (a, b) in enumerate(zip(sources, held))]
-    for load in loads:
-        load.start()
 
     barrier = pltpu.get_barrier_semaphore()
+    groups = nodes // RING
+    group, place = node // RING, lax.rem(node, RING)
 
     def greet_lane(k, _):
         pl.semaphore_signal(barrier, inc=1, device_id=(lax.rem(lane + k, lanes), node), device_id_type=MESH)
         return 0
 
-    def greet_node(k, _):
-        pl.semaphore_signal(barrier, inc=1, device_id=(lane, lax.rem(node + k, nodes)), device_id_type=MESH)
+    def greet_ring(k, _):
+        to = group * RING + lax.rem(place + k, RING)
+        pl.semaphore_signal(barrier, inc=1, device_id=(lane, to), device_id_type=MESH)
         return 0
 
+    def greet_group(semaphore):
+        def greet(k, _):
+            to = lax.rem(group + k, groups) * RING + place
+            pl.semaphore_signal(semaphore, inc=1, device_id=(lane, to), device_id_type=MESH)
+            return 0
+
+        lax.fori_loop(1, groups, greet, 0)
+
+    lax.fori_loop(1, RING, greet_ring, 0)
+    greet_group(barrier)
     lax.fori_loop(1, lanes, greet_lane, 0)
-    lax.fori_loop(1, nodes, greet_node, 0)
+    for load in loads:
+        load.start()
 
     for load in loads[:6]:
         load.wait()
@@ -91,8 +105,7 @@
     for o in range(nodes):
         asked_out[o, :, 0:cap] = requests[o : o + 1, :]
     asked_in[pl.ds(node, 1), :, 0:cap] = asked_out[pl.ds(node, 1), :, 0:cap]
-    lane_source[pl.ds(lane, 1)] = source_ref[...][None]
-    lane_bucket[pl.ds(lane, 1)] = bucket_ref[...][None]
+    lane_event[pl.ds(lane, 1)] = event_ref[...][None]
     te = frequency_ref.shape[1]
     frequency = jnp.broadcast_to(frequency_ref[...], (te, te)).T
     phase = jnp.broadcast_to(phase_ref[...], (te, te)).T
@@ -100,20 +113,17 @@
     for j in range(neighbours):
         enc[j] = cosine(frequency * ages[j : j + 1, :] + phase)
     node_row = lax.broadcasted_iota(jnp.int32, (owned, events), 0)
-    own_member = (node_row == source_ref[...]).astype(F32)
+    own_member = (node_row == event_ref[0:1, :]).astype(F32)
     picker = own_member.T.astype(BF16)
 
-    pl.semaphore_wait(barrier, lanes - 1 + nodes - 1)
-
-    def lane_copies(k):
+    pl.semaphore_wait(barrier, lanes - 1 + RING - 1 + groups - 1)
+
+    def lane_copy(k):
         to = lax.rem(lane + k, lanes)
-        return [
-            pltpu.make_async_remote_copy(
-                src_ref=ref, dst_ref=held.at[lane], send_sem=lane_send.at[i, k], recv_sem=lane_recv.at[i, k],
-                device_id=(to, node), device_id_type=MESH,
-            )
-            for i, (ref, held) in enumerate(((source_ref, lane_source), (bucket_ref, lane_bucket)))
-        ]
+        return pltpu.make_async_remote_copy(
+            src_ref=event_ref, dst_ref=lane_event.at[lane], send_sem=lane_send.at[k], recv_sem=lane_recv.at[k],
+            device_id=(to, node), device_id_type=MESH,
+        )
 
     def ask_copy(k):
         to = lax.rem(node + k, nodes)
@@ -125,7 +135,7 @@
     def row_copy(k):
         to = lax.rem(node + k, nodes)
         return pltpu.make_async_remote_copy(
-            src_ref=send_buf.at[to], dst_ref=far.at[node], send_sem=row_send.at[k], recv_sem=row_recv.at[k],
+            src_ref=send_buf.at[to], dst_ref=far.at[k], send_sem=row_send.at[k], recv_sem=row_recv.at[k],
             device_id=(lane, to), device_id_type=MESH,
         )
 
@@ -136,17 +146,23 @@
 
         lax.fori_loop(1, count, step, 0)
 
-    loop(lanes, lambda k: [copy.start() for copy in lane_copies(k)])
+    def wait_row(k, _):
+        row_copy(k).wait()
+        return 0
+
+    loop(lanes, lambda k: lane_copy(k).start())
+    greet_group(met)
+    pl.semaphore_wait(met, groups - 1)
     loop(nodes, lambda k: ask_copy(k).start())
-    loop(lanes, lambda k: [copy.wait() for copy in lane_copies(k)])
+    loop(lanes, lambda k: lane_copy(k).wait())
 
     for load in loads[6:11]:
         load.wait()
     ones = jnp.ones((te, events), BF16)
     sums = []
     for l in range(lanes):
-        member = (node_row == lane_source[l]).astype(F32)
-        encoded = cosine(frequency * lane_bucket[l].astype(F32) + phase)
+        member = (node_row == lane_event[l, 0:1, :]).astype(F32)
+        encoded = cosine(frequency * lane_event[l, 1:2, :].astype(F32) + phase)
         sums.append(nt(member, encoded, EXACT))
         touched[l] = nt(member.astype(BF16), ones)
     summed[...] = nn(jnp.concatenate(sums, axis=0), wm[...], EXACT).reshape(lanes, owned, channels)
@@ -168,7 +184,7 @@
     picks = jnp.concatenate([(asked[0:cap, o : o + 1] == node_lane).astype(F32) for o in range(nodes)], axis=0)
     send_buf[...] = nn(picks.astype(BF16), rows).astype(BF16).reshape(nodes, cap, channels)
     loop(nodes, lambda k: row_copy(k).start())
-    far[pl.ds(node, 1)] = send_buf[pl.ds(node, 1)]
+    far[0:1] = send_buf[pl.ds(node, 1)]
 
     for load in loads[11:]:
         load.wait()
@@ -190,30 +206,36 @@
         )
     acc[...] = jnp.zeros_like(acc)
 
-    loop(nodes, lambda k: row_copy(k).wait())
-    table = far[...].reshape(total, channels)
-    value[0:total, :] = nn(table, wkv[:, width:]).astype(BF16)
-    score[...] = nt(table, qk[...])
+    distance = node - lax.shift_right_logical(slot_ref[...], shift)
+    distance = jnp.where(distance < 0, distance + nodes, distance)
+    slot_ref[...] = distance * cap + (slot_ref[...] & (cap - 1))
 
     piece = 32
+    part = RING * cap
     piece_row = lax.broadcasted_iota(jnp.int32, (piece, events), 0)
 
-    def gather(c, _):
-        base = pl.multiple_of(c * piece, piece)
-        for j in range(neighbours):
-            hit = (piece_row + base) == slot_ref[j : j + 1, :]
-            for h in range(HEADS):
-                found = jnp.where(hit, score[pl.ds(base, piece), h * events : (h + 1) * events], 0.0)
-                acc[h, j] += jnp.sum(found.reshape(piece // 8, 8, events), axis=0)
-        return 0
-
-    lax.fori_loop(0, total // piece, gather, 0)
+    for c in range(nodes // RING):
+        lax.fori_loop(max(1, c * RING), (c + 1) * RING, wait_row, 0)
+        table = far[c * RING : (c + 1) * RING].reshape(part, channels)
+        score[...] = nt(table, qk[...])
+
+        def gather(p, _, c=c):
+            base = pl.multiple_of(p * piece, piece)
+            for j in range(neighbours):
+                hit = (piece_row + (base + c * part)) == slot_ref[j : j + 1, :]
+                for h in range(HEADS):
+                    found = jnp.where(hit, score[pl.ds(base, piece), h * events : (h + 1) * events], 0.0)
+                    acc[h, j] += jnp.sum(found.reshape(piece // 8, 8, events), axis=0)
+            return 0
+
+        lax.fori_loop(0, part // piece, gather, 0)
+        value[c * part : (c + 1) * part, :] = nn(table, wkv[:, width:]).astype(BF16)
     for h in range(HEADS):
         for j in range(neighbours):
             scores[h, j : j + 1, :] = jnp.sum(acc[h, j], axis=0, keepdims=True)
     logits = (scores[...] + timed[...]) * (1.0 / math.sqrt(size))
-    place = lax.broadcasted_iota(jnp.int32, logits.shape, 1)
-    valid = (place < count_ref[...][None]) | (place == neighbours)
+    order = lax.broadcasted_iota(jnp.int32, logits.shape, 1)
+    valid = (order < count_ref[...][None]) | (order == neighbours)
     logits = jnp.where(valid, logits, -1e30)
     expo = jnp.where(valid, jnp.exp(logits - jnp.max(logits, axis=1, keepdims=True)), 0.0)
     scores[...] = (expo / jnp.sum(expo, axis=1, keepdims=True)).astype(BF16).astype(F32)
@@ -285,8 +307,7 @@
         in_specs=[hbm] * 15,
         out_specs=(vmem, vmem, vmem),
         scratch_shapes=[
-            pltpu.VMEM((1, events), jnp.int32),
-            pltpu.VMEM((1, events), jnp.int32),
+            pltpu.VMEM((2, events), jnp.int32),
             pltpu.VMEM((cap, nodes), jnp.int32),
             pltpu.VMEM((1, te), F32),
             pltpu.VMEM((1, te), F32),
@@ -301,8 +322,7 @@
             pltpu.VMEM(weight_time.shape, BF16),
             pltpu.VMEM(weight_skip.shape, BF16),
             dma((15,)),
-            pltpu.VMEM((lanes, 1, events), jnp.int32),
-            pltpu.VMEM((lanes, 1, events), jnp.int32),
+            pltpu.VMEM((lanes, 2, events), jnp.int32),
             pltpu.VMEM((nodes, 1, 128), jnp.int32),
             pltpu.VMEM((nodes, 1, 128), jnp.int32),
             pltpu.VMEM((nodes, cap, channels), BF16),
@@ -315,15 +335,16 @@
             pltpu.VMEM((HEADS, 16, events), F32),
             pltpu.VMEM((owned, channels), BF16),
             pltpu.VMEM((total + owned, width), BF16),
-            pltpu.VMEM((total, HEADS * events), F32),
+            pltpu.VMEM((RING * cap, HEADS * events), F32),
             pltpu.VMEM((total + owned, HEADS * events), BF16),
             pltpu.VMEM((HEADS * events, channels), BF16),
-            dma((2, lanes)),
-            dma((2, lanes)),
+            dma((lanes,)),
+            dma((lanes,)),
             dma((nodes,)),
             dma((nodes,)),
             dma((nodes,)),
             dma((nodes,)),
+            pltpu.SemaphoreType.REGULAR,
         ],
         compiler_params=pltpu.CompilerParams(
             collective_id=0, has_side_effects=True, vmem_limit_bytes=56 * 1024 * 1024

time: 42.1 us -> 40 us (0.950)
  the two profiles are of different devices: /device:TPU:1 before, /device:TPU:16 now
where the time goes in v3:
time: 40 us; the launch traced here: 39.9 us
  Pallas kernels  39.2 us (98%)
  between operations  0.64 us (2%)
    pallas_call x1, Pallas kernels, local(): pl.pallas_call(functools.partial(kernel, lanes, nodes), out_shape=(jax.Sh...  36.3 us
    pallas_call x1, Pallas kernels, local(): pl.pallas_call(finish, out_shape=(jax.ShapeDtypeStruct((events, width), B...  2.89 us

profile of v3, /device:TPU:16, one launch (start us, length us, event | category | flops | bytes accessed | tf_op | source)
XLA Modules:
  0.0 39.9 jit_solution(17456952637775933998)
XLA Ops:
  0.6 36.3 %shard_map.167 = (bf16[128,1024]{1,0:T(8,128)(2,1)}, f32[128,1024]{1,0:T(8,128)}, f32[64,512]{1,0:T(8,128)}) custom-call(s32[1,128]{1,0:T(1,128)} %bitcast.14, s32[1,128]{1,0:T(1,128)} %bitcast.15, s32[16,32]{1,0:T(8,128)} %bitcast.10, f32[1,128]{1,0:T(1,128)} %bitcast.16, f32[1,128]{1,0:T(1,128)} %bitcast.17, s32[10,128]{1,0:T(8,128)} %bitcast.11, ...), custom_call_target="tpu_custom_call" | custom-call | tf_op jit(solution)/shard_map/pallas_call | solution.py:300
  37.0 2.9 %shard_map.168 = (bf16[128,1024]{1,0:T(8,128)(2,1)}, f32[64,512]{1,0:T(8,128)}) custom-call(bf16[128,1024]{1,0:T(8,128)(2,1)} %get-tuple-element.7.attended_hbm, f32[128,1024]{1,0:T(8,128)} %get-tuple-element.8.base_hbm, f32[64,512]{1,0:T(8,128)} %get-tuple-element.9.memory_hbm, bf16[1024,1024]{1,0:T(8,128)(2,1)} %output_hbm.1), custom_call_target="tpu_custom_call" | custom-call | tf_op jit(solution)/shard_map/pallas_call | solution.py:357

commit v4 on v3

--- a/solution.py
+++ b/solution.py
@@ -12,7 +12,6 @@
 HEADS = 8
 RING = 8
 F32, BF16 = jnp.float32, jnp.bfloat16
-EXACT = lax.Precision.HIGHEST
 SINE = (0.5, -0.020833322778344154, 0.0002604078035801649, -1.5475785630769678e-06, 5.088033105948853e-09)
 TURN_HIGH = 6.28125
 TURN_LOW = 2.0 * math.pi - TURN_HIGH
@@ -30,12 +29,12 @@
     return 1.0 - 2.0 * (half * half)
 
 
-def nn(a, b, precision=None):
-    return lax.dot_general(a, b, (((1,), (0,)), ((), ())), precision=precision, preferred_element_type=F32)
-
-
-def nt(a, b, precision=None):
-    return lax.dot_general(a, b, (((1,), (1,)), ((), ())), precision=precision, preferred_element_type=F32)
+def nn(a, b):
+    return lax.dot_general(a, b, (((1,), (0,)), ((), ())), preferred_element_type=F32)
+
+
+def nt(a, b):
+    return lax.dot_general(a, b, (((1,), (1,)), ((), ())), preferred_element_type=F32)
 
 
 def tn(a, b):
@@ -104,7 +103,7 @@
     requests = request_ref[...].T
     for o in range(nodes):
         asked_out[o, :, 0:cap] = requests[o : o + 1, :]
-    asked_in[pl.ds(node, 1), :, 0:cap] = asked_out[pl.ds(node, 1), :, 0:cap]
+    asked_in[0:1, :, 0:cap] = asked_out[pl.ds(node, 1), :, 0:cap]
     lane_event[pl.ds(lane, 1)] = event_ref[...][None]
     te = frequency_ref.shape[1]
     frequency = jnp.broadcast_to(frequency_ref[...], (te, te)).T
@@ -128,14 +127,14 @@
     def ask_copy(k):
         to = lax.rem(node + k, nodes)
         return pltpu.make_async_remote_copy(
-            src_ref=asked_out.at[to], dst_ref=asked_in.at[node], send_sem=ask_send.at[k], recv_sem=ask_recv.at[k],
+            src_ref=asked_out.at[to], dst_ref=asked_in.at[k], send_sem=ask_send.at[k], recv_sem=ask_recv.at[k],
             device_id=(lane, to), device_id_type=MESH,
         )
 
     def row_copy(k):
-        to = lax.rem(node + k, nodes)
+        to = lax.rem(node + nodes - k, nodes)
         return pltpu.make_async_remote_copy(
-            src_ref=send_buf.at[to], dst_ref=far.at[k], send_sem=row_send.at[k], recv_sem=row_recv.at[k],
+            src_ref=send_buf.at[k], dst_ref=far.at[k], send_sem=row_send.at[k], recv_sem=row_recv.at[k],
             device_id=(lane, to), device_id_type=MESH,
         )
 
@@ -147,8 +146,20 @@
         lax.fori_loop(1, count, step, 0)
 
     def wait_row(k, _):
-        row_copy(k).wait()
-        return 0
+        row_copy(k).wait_recv()
+        return 0
+
+    def start_row(k, _):
+        row_copy(k).start()
+        return 0
+
+    def wait_ask(k, _):
+        ask_copy(k).wait_recv()
+        return 0
+
+    def sent(k):
+        ask_copy(k).wait_send()
+        row_copy(k).wait_send()
 
     loop(lanes, lambda k: lane_copy(k).start())
     greet_group(met)
@@ -161,11 +172,11 @@
     ones = jnp.ones((te, events), BF16)
     sums = []
     for l in range(lanes):
-        member = (node_row == lane_event[l, 0:1, :]).astype(F32)
+        member = (node_row == lane_event[l, 0:1, :]).astype(F32).astype(BF16)
         encoded = cosine(frequency * lane_event[l, 1:2, :].astype(F32) + phase)
-        sums.append(nt(member, encoded, EXACT))
-        touched[l] = nt(member.astype(BF16), ones)
-    summed[...] = nn(jnp.concatenate(sums, axis=0), wm[...], EXACT).reshape(lanes, owned, channels)
+        sums.append(nt(member, encoded.astype(BF16)))
+        touched[l] = nt(member, ones)
+    summed[...] = nn(jnp.concatenate(sums, axis=0).astype(BF16), wm[...].astype(BF16)).reshape(lanes, owned, channels)
     decay = -decay_ref[...]
     state = start_ref[...]
 
@@ -178,13 +189,15 @@
     rows = state.astype(BF16)
     table_own[...] = rows
 
-    loop(nodes, lambda k: ask_copy(k).wait())
-    asked = jnp.concatenate([asked_in[o, :, :] for o in range(nodes)], axis=0).T
     node_lane = lax.broadcasted_iota(jnp.int32, (cap, owned), 1)
-    picks = jnp.concatenate([(asked[0:cap, o : o + 1] == node_lane).astype(F32) for o in range(nodes)], axis=0)
-    send_buf[...] = nn(picks.astype(BF16), rows).astype(BF16).reshape(nodes, cap, channels)
-    loop(nodes, lambda k: row_copy(k).start())
-    far[0:1] = send_buf[pl.ds(node, 1)]
+    for c in range(nodes // RING):
+        near, past = c * RING, (c + 1) * RING
+        lax.fori_loop(max(1, near), past, wait_ask, 0)
+        asked = jnp.concatenate([asked_in[o, :, :] for o in range(near, past)], axis=0).T
+        picks = jnp.concatenate([(asked[0:cap, o : o + 1] == node_lane).astype(F32) for o in range(RING)], axis=0)
+        send_buf[near:past] = nn(picks.astype(BF16), rows).astype(BF16).reshape(RING, cap, channels)
+        lax.fori_loop(max(1, near), past, start_row, 0)
+    far[0:1] = send_buf[0:1]
 
     for load in loads[11:]:
         load.wait()
@@ -206,7 +219,7 @@
         )
     acc[...] = jnp.zeros_like(acc)
 
-    distance = node - lax.shift_right_logical(slot_ref[...], shift)
+    distance = lax.shift_right_logical(slot_ref[...], shift) - node
     distance = jnp.where(distance < 0, distance + nodes, distance)
     slot_ref[...] = distance * cap + (slot_ref[...] & (cap - 1))
 
@@ -230,6 +243,7 @@
 
         lax.fori_loop(0, part // piece, gather, 0)
         value[c * part : (c + 1) * part, :] = nn(table, wkv[:, width:]).astype(BF16)
+    loop(nodes, sent)
     for h in range(HEADS):
         for j in range(neighbours):
             scores[h, j : j + 1, :] = jnp.sum(acc[h, j], axis=0, keepdims=True)

time: 40 us -> 39.3 us (0.982)
  the two profiles are of different devices: /device:TPU:16 before, /device:TPU:32 now
where the time goes in v4:
time: 39.3 us; the launch traced here: 39.1 us
  Pallas kernels  38.5 us (98%)
  between operations  0.64 us (2%)
    pallas_call x1, Pallas kernels, local(): pl.pallas_call(functools.partial(kernel, lanes, nodes), out_shape=(jax.Sh...  35.6 us
    pallas_call x1, Pallas kernels, local(): pl.pallas_call(finish, out_shape=(jax.ShapeDtypeStruct((events, width), B...  2.89 us

profile of v4, /device:TPU:32, one launch (start us, length us, event | category | flops | bytes accessed | tf_op | source)
XLA Modules:
  0.0 39.1 jit_solution(1596780209003826968)
XLA Ops:
  0.6 35.6 %shard_map.167 = (bf16[128,1024]{1,0:T(8,128)(2,1)}, f32[128,1024]{1,0:T(8,128)}, f32[64,512]{1,0:T(8,128)}) custom-call(s32[1,128]{1,0:T(1,128)} %bitcast.14, s32[1,128]{1,0:T(1,128)} %bitcast.15, s32[16,32]{1,0:T(8,128)} %bitcast.10, f32[1,128]{1,0:T(1,128)} %bitcast.16, f32[1,128]{1,0:T(1,128)} %bitcast.17, s32[10,128]{1,0:T(8,128)} %bitcast.11, ...), custom_call_target="tpu_custom_call" | custom-call | tf_op jit(solution)/shard_map/pallas_call | solution.py:314
  36.3 2.9 %shard_map.168 = (bf16[128,1024]{1,0:T(8,128)(2,1)}, f32[64,512]{1,0:T(8,128)}) custom-call(bf16[128,1024]{1,0:T(8,128)(2,1)} %get-tuple-element.7.attended_hbm, f32[128,1024]{1,0:T(8,128)} %get-tuple-element.8.base_hbm, f32[64,512]{1,0:T(8,128)} %get-tuple-element.9.memory_hbm, bf16[1024,1024]{1,0:T(8,128)(2,1)} %output_hbm.1), custom_call_target="tpu_custom_call" | custom-call | tf_op jit(solution)/shard_map/pallas_call | solution.py:371
